TPU v7x, 32 devices: a whole 2x2x4 slice. The times are simulated.
32 devices in a mesh: groups: 2 (over y), ctx: 4 (over z), chan: 4 (over x, core).
Axes of the slice: x: 2, y: 2, z: 4, core: 2. Of those that a mesh axis runs over, the one named last changes fastest.
Arguments:
- projections: bfloat16 [3, 256, 16384], P(None, ('groups', 'chan'), 'ctx'), parts along dimension 1, may hold values from -6 to 6
- short_weights: float32 [3, 3, 256], P(None, None, ('groups', 'chan')), parts along dimension 2, may hold values from -3.5 to 3.5
- residues: float32 [256, 16], P(('groups', 'chan')), parts along dimension 0, may hold values from -4 to 4
- rates: float32 [256, 16], P(('groups', 'chan')), parts along dimension 0, may hold values from 0.25 to 512
- skip: float32 [256], P(('groups', 'chan')), parts along dimension 0, may hold values from -3 to 3
Outputs:
- mixer_out: bfloat16 [256, 16384], P(('groups', 'chan'), 'ctx'), parts along dimension 0
There are 2 independent parts, one for each index of `groups`. A program takes and returns all parts, laid end to end along the dimension named above; each array names one. Nothing has to cross between parts.
All inputs are finite; a program needn't handle non-finite values.
Results may differ from a plain program's by a relative error of at most 0.0065.
Values may be sent and summed in bfloat16 or wider, within the bound.
A program may use at most 64 MiB of HBM per device.

v0:
```python
import functools

import jax
import jax.numpy as jnp
from jax import lax
from jax.experimental import pallas as pl
from jax.experimental.pallas import tpu as pltpu
from jax.sharding import PartitionSpec as P

LANES = 128


def column(row):
    size = row.shape[1]
    r = lax.broadcasted_iota(jnp.int32, (size, size), 0)
    c = lax.broadcasted_iota(jnp.int32, (size, size), 1)
    spread = jnp.where(r == c, jnp.broadcast_to(row, (size, size)), 0.0)
    return jnp.sum(spread, axis=1, keepdims=True)


def short_block(cur, prev, taps, lane):
    one = jnp.where(lane < 1, pltpu.roll(prev, 1, 1), pltpu.roll(cur, 1, 1))
    two = jnp.where(lane < 2, pltpu.roll(prev, 2, 1), pltpu.roll(cur, 2, 1))
    total = taps[0] * cur + taps[1] * one + taps[2] * two
    return total.astype(jnp.bfloat16).astype(jnp.float32)


def kernel(n, unroll, p_hbm, sw_ref, res_ref, rate_ref, skip_ref, o_hbm,
           pbuf, rim, u, y, e_tab, g_tab, f_tab, s_tab, snd, rcv, obuf,
           in_sems, rim_send, rim_recv, st_send, st_recv, out_sems):
    me = lax.axis_index("ctx")
    _, ch, length = pbuf.shape
    modes = res_ref.shape[1]
    blocks = length // LANES
    seq = n * length

    copies = [
        pltpu.make_async_copy(p_hbm.at[i], pbuf.at[i], in_sems.at[i]) for i in range(3)
    ]
    for i in (1, 2, 0):
        copies[i].start()

    if n > 1:
        barrier = pltpu.get_barrier_semaphore()
        for k in range(1, n):
            pl.semaphore_signal(
                barrier, inc=1, device_id={"ctx": lax.rem(me + k, n)},
                device_id_type=pl.DeviceIdType.MESH,
            )
        pl.semaphore_wait(barrier, n - 1)

    rim_copy = pltpu.make_async_remote_copy(
        src_ref=p_hbm.at[:, :, pl.ds(length - LANES, LANES)],
        dst_ref=rim,
        send_sem=rim_send,
        recv_sem=rim_recv,
        device_id={"ctx": lax.rem(me + 1, n)},
        device_id_type=pl.DeviceIdType.MESH,
    )

    @pl.when(me + 1 < n)
    def _():
        rim_copy.start()

    lane = lax.broadcasted_iota(jnp.int32, (ch, LANES), 1)
    pos = lane.astype(jnp.float32)
    rate = rate_ref[...] / seq
    coef = res_ref[...] * jnp.sqrt(2.0 * rate / modes)
    step_decay = jnp.exp(-(rate * LANES))

    filt = jnp.zeros((ch, LANES), jnp.float32)
    for m in range(modes):
        d = rate[:, m : m + 1]
        a = coef[:, m : m + 1]
        e_tab[pl.ds(m * ch, ch), :] = jnp.exp(-(d * (LANES - 1.0 - pos)))
        filt = filt + a * jnp.exp(-(d * pos))
        g_tab[pl.ds(m * ch, ch), :] = a * jnp.exp(-(d * (pos + 1.0)))
    f_tab[...] = filt

    taps = [
        [jnp.broadcast_to(column(sw_ref[i, j : j + 1, :]), (ch, LANES)) for j in range(3)]
        for i in range(3)
    ]
    skip_col = jnp.broadcast_to(column(skip_ref[...]), (ch, LANES))

    def tile(i, b):
        at = pl.multiple_of(b * LANES, LANES)
        return pbuf[i, :, pl.ds(at, LANES)].astype(jnp.float32)

    copies[1].wait()
    copies[2].wait()

    def mix(b, prev):
        k, v = tile(1, b), tile(2, b)
        ks = short_block(k, prev[0], taps[1], lane)
        vs = short_block(v, prev[1], taps[2], lane)
        u[pl.ds(pl.multiple_of(b * ch, ch), ch), :] = ks * vs
        return k, v

    lax.fori_loop(1, blocks, mix, (tile(1, 0), tile(2, 0)), unroll=False)

    @pl.when(me > 0)
    def _():
        rim_copy.wait_recv()

    @pl.when(me == 0)
    def _():
        rim[...] = jnp.zeros(rim.shape, rim.dtype)

    mix(0, (rim[1].astype(jnp.float32), rim[2].astype(jnp.float32)))

    def states(i, carry):
        for j in range(unroll):
            c = i * unroll + j
            uc = u[pl.ds(c, blocks, stride=ch), :].astype(jnp.bfloat16)
            ec = e_tab[pl.ds(c, modes, stride=ch), :].astype(jnp.bfloat16)
            s_tab[pl.ds(c, blocks, stride=ch), pl.ds(0, modes)] = lax.dot_general(
                uc, ec, (((1,), (1,)), ((), ())), preferred_element_type=jnp.float32
            )
        return carry

    lax.fori_loop(0, ch // unroll, states, 0)

    def local(b, h):
        return h * step_decay + s_tab[pl.ds(pl.multiple_of(b * ch, ch), ch), pl.ds(0, modes)]

    snd[...] = lax.fori_loop(0, blocks, local, jnp.zeros((ch, modes), jnp.float32), unroll=8)

    sends = [
        pltpu.make_async_remote_copy(
            src_ref=snd,
            dst_ref=rcv.at[k - 1],
            send_sem=st_send.at[k - 1],
            recv_sem=st_recv.at[k - 1],
            device_id={"ctx": lax.rem(me + k, n)},
            device_id_type=pl.DeviceIdType.MESH,
        )
        for k in range(1, n)
    ]
    for k in range(1, n):
        @pl.when(me + k < n)
        def _():
            sends[k - 1].start()

    row = lax.broadcasted_iota(jnp.int32, (LANES, LANES), 0)
    col = lax.broadcasted_iota(jnp.int32, (LANES, LANES), 1)
    causal = col >= row

    def intra(i, carry):
        for j in range(unroll):
            c = i * unroll + j
            uc = u[pl.ds(c, blocks, stride=ch), :].astype(jnp.bfloat16)
            spread = jnp.broadcast_to(f_tab[pl.ds(c, 1), :], (LANES, LANES))
            spread = pltpu.roll(spread, 0, 1, stride=1, stride_axis=0)
            toep = jnp.where(causal, spread, 0.0).astype(jnp.bfloat16)
            y[pl.ds(c, blocks, stride=ch), :] = jnp.dot(
                uc, toep, preferred_element_type=jnp.float32
            )
        return carry

    lax.fori_loop(0, ch // unroll, intra, 0)

    for k in range(1, n):
        @pl.when(me >= k)
        def _():
            sends[k - 1].wait_recv()

        @pl.when(me < k)
        def _():
            rcv[k - 1] = jnp.zeros((ch, modes), jnp.float32)

    h0 = jnp.zeros((ch, modes), jnp.float32)
    for k in range(1, n):
        h0 = h0 + rcv[k - 1] * jnp.exp(-(rate * float(length * (k - 1))))

    def scan(b, h):
        at = pl.ds(pl.multiple_of(b * ch, ch), ch)
        s = s_tab[at, pl.ds(0, modes)]
        s_tab[at, pl.ds(0, modes)] = h
        return h * step_decay + s

    lax.fori_loop(0, blocks, scan, h0, unroll=8)

    def inter(i, carry):
        for j in range(unroll):
            c = i * unroll + j
            hc = s_tab[pl.ds(c, blocks, stride=ch), pl.ds(0, modes)].astype(jnp.bfloat16)
            gc = g_tab[pl.ds(c, modes, stride=ch), :].astype(jnp.bfloat16)
            y[pl.ds(c, blocks, stride=ch), :] += jnp.dot(
                hc, gc, preferred_element_type=jnp.float32
            )
        return carry

    lax.fori_loop(0, ch // unroll, inter, 0)

    copies[0].wait()

    def gate(b, prev):
        q = tile(0, b)
        qs = short_block(q, prev, taps[0], lane)
        at = pl.ds(pl.multiple_of(b * ch, ch), ch)
        value = qs * (y[at, :] + skip_col * u[at, :])
        obuf[:, pl.ds(pl.multiple_of(b * LANES, LANES), LANES)] = value.astype(obuf.dtype)
        return q

    pieces = out_sems.shape[0]
    per = blocks // pieces
    prev = rim[0].astype(jnp.float32)
    outs = []
    for piece in range(pieces):
        prev = lax.fori_loop(piece * per, (piece + 1) * per, gate, prev, unroll=False)
        span = pl.ds(piece * per * LANES, per * LANES)
        outs.append(
            pltpu.make_async_copy(obuf.at[:, span], o_hbm.at[:, span], out_sems.at[piece])
        )
        outs[-1].start()

    @pl.when(me + 1 < n)
    def _():
        rim_copy.wait_send()

    for k in range(1, n):
        @pl.when(me + k < n)
        def _():
            sends[k - 1].wait_send()

    for out in outs:
        out.wait()


def shards(projections, short_weights, residues, rates, skip):
    n = lax.axis_size("ctx")
    _, ch, length = projections.shape
    modes = residues.shape[1]
    blocks = length // LANES
    vmem = pl.BlockSpec(memory_space=pltpu.VMEM)
    hbm = pl.BlockSpec(memory_space=pl.ANY)
    return pl.pallas_call(
        functools.partial(kernel, n, 8),
        out_shape=jax.ShapeDtypeStruct((ch, length), jnp.bfloat16),
        in_specs=[hbm, vmem, vmem, vmem, vmem],
        out_specs=hbm,
        scratch_shapes=[
            pltpu.VMEM((3, ch, length), jnp.bfloat16),
            pltpu.VMEM((3, ch, LANES), jnp.bfloat16),
            pltpu.VMEM((blocks * ch, LANES), jnp.float32),
            pltpu.VMEM((blocks * ch, LANES), jnp.float32),
            pltpu.VMEM((modes * ch, LANES), jnp.float32),
            pltpu.VMEM((modes * ch, LANES), jnp.float32),
            pltpu.VMEM((ch, LANES), jnp.float32),
            pltpu.VMEM((blocks * ch, LANES), jnp.float32),
            pltpu.VMEM((ch, modes), jnp.float32),
            pltpu.VMEM((n - 1, ch, modes), jnp.float32),
            pltpu.VMEM((ch, length), jnp.bfloat16),
            pltpu.SemaphoreType.DMA((3,)),
            pltpu.SemaphoreType.DMA,
            pltpu.SemaphoreType.DMA,
            pltpu.SemaphoreType.DMA((n - 1,)),
            pltpu.SemaphoreType.DMA((n - 1,)),
            pltpu.SemaphoreType.DMA((4,)),
        ],
        compiler_params=pltpu.CompilerParams(
            collective_id=0, has_side_effects=True, vmem_limit_bytes=32 * 1024 * 1024
        ),
        name="mixer",
    )(projections, short_weights, residues, rates, skip[None, :])


def solution(mesh):
    return jax.shard_map(
        shards,
        mesh=mesh,
        in_specs=(
            P(None, ("groups", "chan"), "ctx"),
            P(None, None, ("groups", "chan")),
            P(("groups", "chan"), None),
            P(("groups", "chan"), None),
            P(("groups", "chan")),
        ),
        out_specs=P(("groups", "chan"), "ctx"),
        check_vma=False,
    )
```

profile of v0, /device:TPU:0, one launch (start us, length us, event | category | flops | bytes accessed | tf_op | source)
XLA Modules:
  0.0 18.7 jit_solution(3789914066734700645)
XLA Ops:
  0.0 0.0 copy-start.3
  0.0 0.8 %copy.6.res_ref = f32[32,16]{1,0:T(8,128)S(1)} copy(f32[32,16]{0,1:T(8,128)} %param.7) | data formatting | bytes 4096 | tf_op args[2]
  0.8 0.0 copy-done.3
  0.8 0.0 copy-start.1
  0.8 0.0 copy-start.2
  0.8 0.1 copy.7.rate_ref
  0.9 0.6 %copy-done.1 = f32[3,3,32]{2,1,0:T(4,128)S(1)} copy-done((f32[3,3,32]{2,1,0:T(4,128)S(1)}, f32[3,3,32]{2,1,0:T(4,128)}, u32[]{:S(2)}) %copy-start.1) | copy-done | bytes 1176
  1.5 0.0 copy-done.2
  1.5 0.0 copy-start
  1.5 1.1 %copy-done = bf16[3,32,4096]{2,1,0:T(8,128)(2,1)S(1)} copy-done((bf16[3,32,4096]{2,1,0:T(8,128)(2,1)S(1)}, bf16[3,32,4096]{2,1,0:T(8,128)(2,1)}, u32[]{:S(2)}) %copy-start) | copy-done | bytes 786456
  2.6 15.3 %mixer.1 = bf16[32,4096]{1,0:T(8,128)(2,1)S(1)} custom-call(bf16[3,32,4096]{2,1,0:T(8,128)(2,1)S(1)} %copy-done, f32[3,3,32]{2,1,0:T(4,128)S(1)} %copy-done.1, f32[32,16]{1,0:T(8,128)S(1)} %copy.6.res_ref, f32[32,16]{1,0:T(8,128)S(1)} %copy.7.rate_ref, f32[1,32]{1,0:T(1,128)S(1)} %bitcast.1), custom_call_target="tpu_custom_call" | custom-call | tf_op jit(solution)/shard_map/mixer/pallas_call | solution.py:238
  18.0 0.7 %copy.9 = bf16[32,4096]{1,0:T(8,128)(2,1)} copy(bf16[32,4096]{1,0:T(8,128)(2,1)S(1)} %mixer.1) | data formatting | bytes 524288
Async XLA Ops:
  0.0 0.8 %copy-start.3 = (f32[32,16]{0,1:T(8,128)S(1)}, f32[32,16]{0,1:T(8,128)}, u32[]{:S(2)}) copy-start(f32[32,16]{0,1:T(8,128)} %param.8) | copy-start | bytes 6148
  0.8 0.7 %copy-start.1 = (f32[3,3,32]{2,1,0:T(4,128)S(1)}, f32[3,3,32]{2,1,0:T(4,128)}, u32[]{:S(2)}) copy-start(f32[3,3,32]{2,1,0:T(4,128)} %sw_ref.1) | copy-start | bytes 3460
  0.8 0.7 %copy-start.2 = (f32[32]{0:T(128)S(1)}, f32[32]{0:T(128)}, u32[]{:S(2)}) copy-start(f32[32]{0:T(128)} %param.9) | copy-start | bytes 388
  1.5 1.1 %copy-start = (bf16[3,32,4096]{2,1,0:T(8,128)(2,1)S(1)}, bf16[3,32,4096]{2,1,0:T(8,128)(2,1)}, u32[]{:S(2)}) copy-start(bf16[3,32,4096]{2,1,0:T(8,128)(2,1)} %p_hbm.1) | copy-start | bytes 2359300
where the time goes:
time: 19 us; the launch traced here: 18.7 us
  Pallas kernels  15.3 us (81%)
  local copies, waits for them, and re-layouts  3.32 us (17%)
    pallas_call x1, Pallas kernels, shards(): pl.pallas_call(functools.partial(kernel, n, 8), out_shape=jax.ShapeDtypeS...  15.3 us
    unnamed x11, local copies, waits for them, and re-layouts  3.32 us

commit v1 on v0

--- a/solution.py
+++ b/solution.py
@@ -25,19 +25,22 @@
     return total.astype(jnp.bfloat16).astype(jnp.float32)
 
 
-def kernel(n, unroll, p_hbm, sw_ref, res_ref, rate_ref, skip_ref, o_hbm,
-           pbuf, rim, u, y, e_tab, g_tab, f_tab, s_tab, snd, rcv, obuf,
-           in_sems, rim_send, rim_recv, st_send, st_recv, out_sems):
+def kernel(n, unroll, p_hbm, sw_hbm, res_hbm, rate_hbm, skip_hbm, o_ref,
+           sw_ref, res_ref, rate_ref, skip_ref, pbuf, rim, u, y, e_tab, g_tab, f_tab, s_tab, p_tab, h_in, snd, rcv,
+           in_sems, rim_send, rim_recv, st_send, st_recv):
     me = lax.axis_index("ctx")
     _, ch, length = pbuf.shape
-    modes = res_ref.shape[1]
+    modes = res_ref.shape[0]
     blocks = length // LANES
     seq = n * length
 
     copies = [
         pltpu.make_async_copy(p_hbm.at[i], pbuf.at[i], in_sems.at[i]) for i in range(3)
     ]
-    for i in (1, 2, 0):
+    small = ((rate_hbm, rate_ref), (res_hbm, res_ref), (sw_hbm, sw_ref), (skip_hbm, skip_ref))
+    for i, (source, target) in enumerate(small):
+        copies.append(pltpu.make_async_copy(source, target, in_sems.at[3 + i]))
+    for i in (3, 4, 5, 6, 1, 2, 0):
         copies[i].start()
 
     if n > 1:
@@ -47,7 +50,6 @@
                 barrier, inc=1, device_id={"ctx": lax.rem(me + k, n)},
                 device_id_type=pl.DeviceIdType.MESH,
             )
-        pl.semaphore_wait(barrier, n - 1)
 
     rim_copy = pltpu.make_async_remote_copy(
         src_ref=p_hbm.at[:, :, pl.ds(length - LANES, LANES)],
@@ -58,14 +60,12 @@
         device_id_type=pl.DeviceIdType.MESH,
     )
 
-    @pl.when(me + 1 < n)
-    def _():
-        rim_copy.start()
-
     lane = lax.broadcasted_iota(jnp.int32, (ch, LANES), 1)
     pos = lane.astype(jnp.float32)
-    rate = rate_ref[...] / seq
-    coef = res_ref[...] * jnp.sqrt(2.0 * rate / modes)
+    for i in (3, 4, 5, 6):
+        copies[i].wait()
+    rate = rate_ref[...].T / seq
+    coef = res_ref[...].T * jnp.sqrt(2.0 * rate / modes)
     step_decay = jnp.exp(-(rate * LANES))
 
     filt = jnp.zeros((ch, LANES), jnp.float32)
@@ -83,6 +83,13 @@
     ]
     skip_col = jnp.broadcast_to(column(skip_ref[...]), (ch, LANES))
 
+    if n > 1:
+        pl.semaphore_wait(barrier, n - 1)
+
+    @pl.when(me + 1 < n)
+    def _():
+        rim_copy.start()
+
     def tile(i, b):
         at = pl.multiple_of(b * LANES, LANES)
         return pbuf[i, :, pl.ds(at, LANES)].astype(jnp.float32)
@@ -97,17 +104,9 @@
         u[pl.ds(pl.multiple_of(b * ch, ch), ch), :] = ks * vs
         return k, v
 
-    lax.fori_loop(1, blocks, mix, (tile(1, 0), tile(2, 0)), unroll=False)
-
-    @pl.when(me > 0)
-    def _():
-        rim_copy.wait_recv()
-
-    @pl.when(me == 0)
-    def _():
-        rim[...] = jnp.zeros(rim.shape, rim.dtype)
-
-    mix(0, (rim[1].astype(jnp.float32), rim[2].astype(jnp.float32)))
+    zero = jnp.zeros((ch, LANES), jnp.float32)
+    lax.fori_loop(0, blocks, mix, (zero, zero), unroll=8)
+    u[pl.ds(0, ch), :] = jnp.where(lane < 2, 0.0, u[pl.ds(0, ch), :])
 
     def states(i, carry):
         for j in range(unroll):
@@ -121,10 +120,31 @@
 
     lax.fori_loop(0, ch // unroll, states, 0)
 
-    def local(b, h):
-        return h * step_decay + s_tab[pl.ds(pl.multiple_of(b * ch, ch), ch), pl.ds(0, modes)]
-
-    snd[...] = lax.fori_loop(0, blocks, local, jnp.zeros((ch, modes), jnp.float32), unroll=8)
+    def local(b, state):
+        h, p = state
+        at = pl.ds(pl.multiple_of(b * ch, ch), ch)
+        s = s_tab[at, pl.ds(0, modes)]
+        s_tab[at, pl.ds(0, modes)] = h
+        p_tab[at, pl.ds(0, modes)] = p
+        return h * step_decay + s, p * step_decay
+
+    first = (jnp.zeros((ch, modes), jnp.float32), jnp.ones((ch, modes), jnp.float32))
+    end, whole = lax.fori_loop(0, blocks, local, first, unroll=8)
+
+    @pl.when(me > 0)
+    def _():
+        rim_copy.wait_recv()
+
+    @pl.when(me == 0)
+    def _():
+        rim[...] = jnp.zeros(rim.shape, rim.dtype)
+
+    mix(0, (rim[1].astype(jnp.float32), rim[2].astype(jnp.float32)))
+    edge = u[pl.ds(0, ch), :]
+    early = jnp.exp(-(rate * (LANES - 1.0))) * edge[:, 0:1] + jnp.exp(
+        -(rate * (LANES - 2.0))
+    ) * edge[:, 1:2]
+    snd[...] = end + jnp.exp(-(rate * float(length - LANES))) * early
 
     sends = [
         pltpu.make_async_remote_copy(
@@ -142,6 +162,13 @@
         def _():
             sends[k - 1].start()
 
+    def add_early(b, p):
+        at = pl.ds(pl.multiple_of(b * ch, ch), ch)
+        s_tab[at, pl.ds(0, modes)] = s_tab[at, pl.ds(0, modes)] + p * early
+        return p_tab[at, pl.ds(0, modes)]
+
+    lax.fori_loop(0, blocks, add_early, jnp.zeros((ch, modes), jnp.float32), unroll=8)
+
     row = lax.broadcasted_iota(jnp.int32, (LANES, LANES), 0)
     col = lax.broadcasted_iota(jnp.int32, (LANES, LANES), 1)
     causal = col >= row
@@ -160,6 +187,17 @@
 
     lax.fori_loop(0, ch // unroll, intra, 0)
 
+    copies[0].wait()
+
+    def ahead(b, prev):
+        q = tile(0, b)
+        at = pl.ds(pl.multiple_of(b * ch, ch), ch)
+        y[at, :] = y[at, :] + skip_col * u[at, :]
+        u[at, :] = short_block(q, prev, taps[0], lane)
+        return q
+
+    lax.fori_loop(0, blocks, ahead, rim[0].astype(jnp.float32), unroll=8)
+
     for k in range(1, n):
         @pl.when(me >= k)
         def _():
@@ -172,19 +210,14 @@
     h0 = jnp.zeros((ch, modes), jnp.float32)
     for k in range(1, n):
         h0 = h0 + rcv[k - 1] * jnp.exp(-(rate * float(length * (k - 1))))
-
-    def scan(b, h):
-        at = pl.ds(pl.multiple_of(b * ch, ch), ch)
-        s = s_tab[at, pl.ds(0, modes)]
-        s_tab[at, pl.ds(0, modes)] = h
-        return h * step_decay + s
-
-    lax.fori_loop(0, blocks, scan, h0, unroll=8)
+    h_in[...] = h0
 
     def inter(i, carry):
         for j in range(unroll):
             c = i * unroll + j
-            hc = s_tab[pl.ds(c, blocks, stride=ch), pl.ds(0, modes)].astype(jnp.bfloat16)
+            hc = s_tab[pl.ds(c, blocks, stride=ch), pl.ds(0, modes)]
+            pc = p_tab[pl.ds(c, blocks, stride=ch), pl.ds(0, modes)]
+            hc = (hc + pc * h_in[pl.ds(c, 1), :]).astype(jnp.bfloat16)
             gc = g_tab[pl.ds(c, modes, stride=ch), :].astype(jnp.bfloat16)
             y[pl.ds(c, blocks, stride=ch), :] += jnp.dot(
                 hc, gc, preferred_element_type=jnp.float32
@@ -193,27 +226,13 @@
 
     lax.fori_loop(0, ch // unroll, inter, 0)
 
-    copies[0].wait()
-
-    def gate(b, prev):
-        q = tile(0, b)
-        qs = short_block(q, prev, taps[0], lane)
+    def gate(b, carry):
         at = pl.ds(pl.multiple_of(b * ch, ch), ch)
-        value = qs * (y[at, :] + skip_col * u[at, :])
-        obuf[:, pl.ds(pl.multiple_of(b * LANES, LANES), LANES)] = value.astype(obuf.dtype)
-        return q
-
-    pieces = out_sems.shape[0]
-    per = blocks // pieces
-    prev = rim[0].astype(jnp.float32)
-    outs = []
-    for piece in range(pieces):
-        prev = lax.fori_loop(piece * per, (piece + 1) * per, gate, prev, unroll=False)
-        span = pl.ds(piece * per * LANES, per * LANES)
-        outs.append(
-            pltpu.make_async_copy(obuf.at[:, span], o_hbm.at[:, span], out_sems.at[piece])
-        )
-        outs[-1].start()
+        value = u[at, :] * y[at, :]
+        o_ref[:, pl.ds(pl.multiple_of(b * LANES, LANES), LANES)] = value.astype(o_ref.dtype)
+        return carry
+
+    lax.fori_loop(0, blocks, gate, 0, unroll=8)
 
     @pl.when(me + 1 < n)
     def _():
@@ -223,9 +242,6 @@
         @pl.when(me + k < n)
         def _():
             sends[k - 1].wait_send()
-
-    for out in outs:
-        out.wait()
 
 
 def shards(projections, short_weights, residues, rates, skip):
@@ -234,13 +250,17 @@
     modes = residues.shape[1]
     blocks = length // LANES
     vmem = pl.BlockSpec(memory_space=pltpu.VMEM)
-    hbm = pl.BlockSpec(memory_space=pl.ANY)
+    hbm = pl.BlockSpec(memory_space=pltpu.HBM)
     return pl.pallas_call(
         functools.partial(kernel, n, 8),
         out_shape=jax.ShapeDtypeStruct((ch, length), jnp.bfloat16),
-        in_specs=[hbm, vmem, vmem, vmem, vmem],
-        out_specs=hbm,
+        in_specs=[hbm] * 5,
+        out_specs=vmem,
         scratch_shapes=[
+            pltpu.VMEM(short_weights.shape, jnp.float32),
+            pltpu.VMEM((modes, ch), jnp.float32),
+            pltpu.VMEM((modes, ch), jnp.float32),
+            pltpu.VMEM((1, ch), jnp.float32),
             pltpu.VMEM((3, ch, length), jnp.bfloat16),
             pltpu.VMEM((3, ch, LANES), jnp.bfloat16),
             pltpu.VMEM((blocks * ch, LANES), jnp.float32),
@@ -249,21 +269,24 @@
             pltpu.VMEM((modes * ch, LANES), jnp.float32),
             pltpu.VMEM((ch, LANES), jnp.float32),
             pltpu.VMEM((blocks * ch, LANES), jnp.float32),
+            pltpu.VMEM((blocks * ch, LANES), jnp.float32),
+            pltpu.VMEM((ch, modes), jnp.float32),
             pltpu.VMEM((ch, modes), jnp.float32),
             pltpu.VMEM((n - 1, ch, modes), jnp.float32),
-            pltpu.VMEM((ch, length), jnp.bfloat16),
-            pltpu.SemaphoreType.DMA((3,)),
+            pltpu.SemaphoreType.DMA((7,)),
             pltpu.SemaphoreType.DMA,
             pltpu.SemaphoreType.DMA,
             pltpu.SemaphoreType.DMA((n - 1,)),
             pltpu.SemaphoreType.DMA((n - 1,)),
-            pltpu.SemaphoreType.DMA((4,)),
         ],
         compiler_params=pltpu.CompilerParams(
             collective_id=0, has_side_effects=True, vmem_limit_bytes=32 * 1024 * 1024
         ),
         name="mixer",
-    )(projections, short_weights, residues, rates, skip[None, :])
+    )(*(
+        pltpu.with_memory_space_constraint(a, pltpu.HBM)
+        for a in (projections, short_weights, residues.T, rates.T, skip[None, :])
+    ))
 
 
 def solution(mesh):

time: 19 us -> 11.4 us (0.60)
  Pallas kernels: 15.3 us -> 10.5 us
  local copies, waits for them, and re-layouts: 3.32 us -> 0.71 us
    pallas_call x1, Pallas kernels: 15.3 us -> 10.5 us  [shards(): pl.pallas_call(functools.partial(kernel, n, 8), out_shape=jax.ShapeDtypeS...]
    unnamed x11 -> x1, local copies, waits for them, and re-layouts: 3.32 us -> 0.71 us
where the time goes in v1:
time: 11.4 us; the launch traced here: 11.2 us
  Pallas kernels  10.5 us (92%)
  local copies, waits for them, and re-layouts  0.71 us (6%)
    pallas_call x1, Pallas kernels, shards(): pl.pallas_call(functools.partial(kernel, n, 8), out_shape=jax.ShapeDtypeS...  10.5 us
    unnamed x1, local copies, waits for them, and re-layouts  0.71 us

profile of v1, /device:TPU:0, one launch (start us, length us, event | category | flops | bytes accessed | tf_op | source)
XLA Modules:
  0.0 11.2 jit_solution(17146898365799791445)
XLA Ops:
  0.0 10.5 %mixer.1 = bf16[32,4096]{1,0:T(8,128)(2,1)S(1)} custom-call(bf16[3,32,4096]{2,1,0:T(8,128)(2,1)} %p_hbm.1, f32[3,3,32]{2,1,0:T(4,128)} %sw_hbm.1, f32[16,32]{1,0:T(8,128)} %bitcast.3, f32[16,32]{1,0:T(8,128)} %bitcast.4, f32[1,32]{1,0:T(1,128)} %bitcast.5), custom_call_target="tpu_custom_call" | custom-call | tf_op jit(solution)/shard_map/mixer/pallas_call | solution.py:254
  10.5 0.7 %copy.7 = bf16[32,4096]{1,0:T(8,128)(2,1)} copy(bf16[32,4096]{1,0:T(8,128)(2,1)S(1)} %mixer.1) | data formatting | bytes 524288
